TPU v7x, 512 devices: a whole 4x8x8 slice. The times are simulated.
512 devices in a mesh: seq: 64 (over y_hi, z, core), tp: 8 (over x, y_lo).
Axes of the slice: x: 4, y: 8 (y_hi: 4, y_lo: 2; y = y_hi * 2 + y_lo), z: 8, core: 2. Of those that a mesh axis runs over, the one named last changes fastest.
Arguments:
- resid: bfloat16 [8192, 2048], P('seq'), may hold values from -1.5 to 1.5
- query: bfloat16 [8192, 1024], P('seq', 'tp'), may hold values from -6 to 6
- key_new: bfloat16 [8192, 1024], P('seq', 'tp'), may hold values from -6 to 6
- value_new: bfloat16 [8192, 1024], P('seq', 'tp'), may hold values from -6 to 6
- key_cache: bfloat16 [1024, 1024], P('seq', 'tp'), may hold values from -6 to 6
- value_cache: bfloat16 [1024, 1024], P('seq', 'tp'), may hold values from -6 to 6
- cache_len: int32 [64], replicated, may hold values from 0 to 16, as said below
- out_weight: bfloat16 [1024, 2048], P('tp'), may hold values from -0.1875 to 0.1875
- norm_gain: bfloat16 [2048], replicated, may hold values from 0.099609375 to 1.8984375
- router: bfloat16 [2048, 64], replicated, may hold values from -2 to 2
- expert_ids: int32 [8192, 6], P('seq'), may hold values from 0 to 63, all different within a row; in each aligned block of 128 rows (0 to 127, 128 to 255, ...) at most 18 rows name the same one
- w_gate: bfloat16 [64, 2048, 1408], P('seq', None, 'tp'), may hold values from -0.125 to 0.125
- w_up: bfloat16 [64, 2048, 1408], P('seq', None, 'tp'), may hold values from -0.125 to 0.125
- w_down: bfloat16 [64, 1408, 2048], P('seq', None, 'tp'), may hold values from -0.15625 to 0.15625
- w_shared_gate: bfloat16 [2048, 1408], P('seq', 'tp'), may hold values from -0.125 to 0.125
- w_shared_up: bfloat16 [2048, 1408], P('seq', 'tp'), may hold values from -0.125 to 0.125
- w_shared_down: bfloat16 [1408, 2048], P('tp', 'seq'), may hold values from -0.15625 to 0.15625
Outputs:
- mixed: bfloat16 [8192, 2048], P('seq', 'tp')
Inputs may be any that keep to these rules, and one draw needn't show every extreme that they name: `cache_len`: some cache block has all 16 rows valid and another has none. `expert_ids`: each row names 6 different experts; the rows of one device name no expert more than 18 times, a bound that some block reaches.
All inputs are finite; a program needn't handle non-finite values.
Results may differ from a plain program's by a relative error of at most 0.013.
Values may be sent and summed in bfloat16 or wider, within the bound.
No kernel may reach another device: no remote copies, remote signals or barrier semaphores. Data moves between devices by JAX's collectives and lax.ppermute only.
A program may use at most 64 MiB of HBM per device.

v0:
```python
import math
import jax
import jax.numpy as jnp
from jax import lax
from jax.sharding import PartitionSpec as P

D = 2048
HD = 128
TOPK = 6


def expert_rows(rows, gate_w, up_w, down_w):
    sources, items = (rows.shape[0], rows.shape[1])
    flat_rows = rows.reshape(sources * items, rows.shape[2])
    gate_pre = jnp.dot(flat_rows, gate_w[0], preferred_element_type=jnp.float32)
    up_pre = jnp.dot(flat_rows, up_w[0], preferred_element_type=jnp.float32)
    inner_units = (
        (jax.nn.silu(gate_pre) * up_pre)
        .astype(jnp.bfloat16)
        .reshape(sources, items, gate_pre.shape[1])
    )
    inner_all = lax.all_gather(inner_units, "tp", axis=2, tiled=True)
    output = jnp.dot(
        inner_all.reshape(sources * items, inner_all.shape[2]),
        down_w[0],
        preferred_element_type=jnp.float32,
    )
    output = output.astype(jnp.bfloat16).reshape(sources, items, down_w.shape[2])
    return lax.all_to_all(output, "seq", split_axis=0, concat_axis=0, tiled=True)


def local(
    resid,
    query,
    key_new,
    value_new,
    key_cache,
    value_cache,
    cache_len,
    out_weight,
    norm_gain,
    router,
    expert_ids,
    w_gate,
    w_up,
    w_down,
    w_shared_gate,
    w_shared_up,
    w_shared_down,
):
    tok_rows = query.shape[0]
    heads_here = query.shape[1] // HD
    block_rows = key_cache.shape[0]
    seq_index = lax.axis_index("seq")
    tp_index = lax.axis_index("tp")
    width = D // lax.axis_size("tp")
    cache_keys, cache_values, fresh_keys, fresh_values = (
        lax.all_gather(key_cache, "seq", axis=0, tiled=True),
        lax.all_gather(value_cache, "seq", axis=0, tiled=True),
        lax.all_gather(key_new, "seq", axis=0, tiled=True),
        lax.all_gather(value_new, "seq", axis=0, tiled=True),
    )
    all_keys = jnp.concatenate([cache_keys, fresh_keys], 0)
    all_values = jnp.concatenate([cache_values, fresh_values], 0)
    span = all_keys.shape[0]
    scores = jnp.einsum(
        "qhd,khd->hqk",
        query.reshape(tok_rows, heads_here, HD),
        all_keys.reshape(span, heads_here, HD),
        preferred_element_type=jnp.float32,
    ) / math.sqrt(HD)
    cache_span = cache_keys.shape[0]
    cache_open = (jnp.arange(block_rows, dtype=jnp.int32)[None, :] < cache_len[:, None]).reshape(
        cache_span
    )
    query_place = seq_index * tok_rows + jnp.arange(tok_rows)
    fresh_open = jnp.arange(fresh_keys.shape[0])[None, :] <= query_place[:, None]
    visible = jnp.concatenate(
        [jnp.broadcast_to(cache_open[None, :], (tok_rows, cache_span)), fresh_open], 1
    )
    scores = jnp.where(visible[None], scores, -jnp.inf)
    top_score = jnp.max(scores, axis=-1, keepdims=True)
    weights = jnp.exp(scores - top_score)
    probs = (weights / jnp.sum(weights, axis=-1, keepdims=True)).astype(jnp.bfloat16)
    attn = jnp.einsum(
        "hqk,khd->qhd",
        probs,
        all_values.reshape(span, heads_here, HD),
        preferred_element_type=jnp.float32,
    )
    attn = attn.astype(jnp.bfloat16).reshape(tok_rows, heads_here * HD)
    partial_out = jnp.dot(attn, out_weight, preferred_element_type=jnp.float32)
    hidden_state = resid.astype(jnp.float32) + lax.psum(partial_out, "tp")
    mean_square = jnp.mean(hidden_state * hidden_state, axis=-1, keepdims=True)
    normed = (hidden_state * lax.rsqrt(mean_square + 1e-06) * norm_gain.astype(jnp.float32)).astype(
        jnp.bfloat16
    )
    own_hidden = lax.dynamic_slice_in_dim(hidden_state, tp_index * width, width, 1)
    logits = jnp.dot(normed, router, preferred_element_type=jnp.float32)
    expert_count = router.shape[1]
    expert_range = jnp.arange(expert_count, dtype=jnp.int32)
    picked = jnp.sum(
        jnp.where(expert_ids[:, :, None] == expert_range[None, None, :], logits[:, None, :], 0.0),
        axis=-1,
    )
    gates = jax.nn.softmax(picked, axis=-1)
    shared_gate = jnp.dot(
        normed,
        lax.all_gather(w_shared_gate, "seq", axis=0, tiled=True),
        preferred_element_type=jnp.float32,
    )
    shared_up = jnp.dot(
        normed,
        lax.all_gather(w_shared_up, "seq", axis=0, tiled=True),
        preferred_element_type=jnp.float32,
    )
    shared_inner = (jax.nn.silu(shared_gate) * shared_up).astype(jnp.bfloat16)
    shared_terms = jnp.dot(
        shared_inner,
        lax.all_gather(w_shared_down, "seq", axis=1, tiled=True),
        preferred_element_type=jnp.float32,
    )
    shared_own = lax.psum_scatter(
        shared_terms.astype(jnp.bfloat16), "tp", scatter_dimension=1, tiled=True
    ).astype(jnp.float32)
    capacity = max(2, 3 * tok_rows * TOPK // (2 * expert_count))
    flat_ids = expert_ids.reshape(tok_rows * TOPK)
    one_hot = (flat_ids[:, None] == expert_range[None, :]).astype(jnp.int32)
    before = jnp.cumsum(one_hot, axis=0) - one_hot
    slot = jnp.sum(one_hot * before, axis=1)
    dest = flat_ids * capacity + slot
    source_row = jnp.repeat(jnp.arange(tok_rows, dtype=jnp.int32), TOPK)
    buffer = jnp.zeros((expert_count * capacity, D), jnp.bfloat16).at[dest].set(normed[source_row])
    buffer = buffer.reshape(expert_count, capacity, D)
    returned = expert_rows(
        lax.all_to_all(buffer, "seq", split_axis=0, concat_axis=0, tiled=True), w_gate, w_up, w_down
    )
    picked_rows = returned.reshape(expert_count * capacity, width)[dest]
    weighted = picked_rows.astype(jnp.float32) * gates.reshape(tok_rows * TOPK)[:, None]
    routed = jnp.sum(weighted.reshape(tok_rows, TOPK, width), axis=1)
    return (own_hidden + shared_own + routed).astype(jnp.bfloat16)


def solution(mesh):
    return jax.shard_map(
        local,
        mesh=mesh,
        in_specs=(
            P("seq", None),
            P("seq", "tp"),
            P("seq", "tp"),
            P("seq", "tp"),
            P("seq", "tp"),
            P("seq", "tp"),
            P(),
            P("tp", None),
            P(),
            P(),
            P("seq", None),
            P("seq", None, "tp"),
            P("seq", None, "tp"),
            P("seq", None, "tp"),
            P("seq", "tp"),
            P("seq", "tp"),
            P("tp", "seq"),
        ),
        out_specs=P("seq", "tp"),
        check_vma=False,
    )
```

profile of v0, /device:TPU:16, one launch (start us, length us, event | category | flops | bytes accessed | tf_op | source)
XLA Modules:
  0.0 870.4 jit_solution(12710250860430260462)
XLA Ops:
  6.5 0.7 all-gather.6.cloned.1.call-update
  7.3 0.7 all-gather.4.cloned.1.call-update
  8.1 0.7 iota_compare_fusion.4
  8.9 76.9 %all_gather.26 = bf16[1024,128]{1,0:T(8,128)(2,1)S(1)} all-gather(bf16[16,128]{1,0:T(8,128)(2,1)} %param.21), channel_id=1, replica_groups=mesh['seq'=64,'tp'=8] {'seq'}, dimensions={0}, use_global_device_ids=true | all-gather | bytes 266240 | tf_op jit(solution)/shard_map/all_gather | solution.py:58
  85.9 75.4 %all_gather.24 = bf16[1024,128]{1,0:T(8,128)(2,1)S(1)} all-gather(bf16[16,128]{1,0:T(8,128)(2,1)} %param.22), channel_id=1, replica_groups=mesh['seq'=64,'tp'=8] {'seq'}, dimensions={0}, use_global_device_ids=true | all-gather | bytes 266240 | tf_op jit(solution)/shard_map/all_gather | solution.py:59
  161.3 0.7 iota_compare_fusion
  162.0 9.6 %fusion.46 = (f32[128]{0:T(128)S(1)}, f32[128,9216]{0,1:T(8,128)S(1)}) fusion(bf16[128,128]{1,0:T(8,128)(2,1)} %param.18, bf16[8192,128]{1,0:T(8,128)(2,1)} %all-gather.6.cloned.1.call-done, bf16[1024,128]{1,0:T(8,128)(2,1)S(1)} %all_gather.26, pred[128,8192]{0,1:T(32,128)(4,1)S(1)} %iota_compare_fusion, pred[9216]{0:T(1024)(128)(4,1)S(1)} %pad.2.clone), kind=kOutput, calls=%fused_computation.71 | convolution fusion | flops 311426944 | bytes 8168960 | tf_op jit(solution)/shard_map/qhd,khd->hqk/dot_general | solution.py:66
  171.6 2.1 copy-done.1
  173.8 1.3 fusion.2
  175.0 8.1 all-gather.4.cloned.1.call-done
  183.2 5.3 fusion.22
  188.7 0.1 eq.42
  188.8 0.1 eq.38
  189.1 0.1 mul.78
  189.3 0.1 reshape.187
  189.4 2.0 reduce-window.6
  191.4 0.3 slice_reduce_fusion
  191.7 0.1 fusion.30
  191.9 89.2 %all-reduce.2.cloned.1.call-done = f32[128,2048]{1,0:T(8,128)} async-done(((f32[128,2048]{1,0:T(8,128)}), f32[128,2048]{1,0:T(8,128)}) %all-reduce.2.cloned.1.call-update) | async-done | bytes 1048592 | tf_op jit(solution)/shard_map/psum | solution.py:93
  281.1 1.4 multiply_reduce_fusion.1
  282.6 0.2 multiply_convert_fusion
  282.8 23.4 %scatter_custom_fusion = bf16[1152,2048]{1,0:T(8,128)(2,1)} fusion(s32[768]{0:T(1024)S(1)} %fusion.40, bf16[128,2048]{1,0:T(8,128)(2,1)S(1)} %multiply_convert_fusion, s32[1024]{0:T(1024)S(1)} %pad_clamp_fusion.1, bf16[]{:T(256)} %constant.44.clone.1), kind=kCustom, calls=%fused_computation.10 | custom fusion | bytes 4718594 | tf_op jit(solution)/shard_map/scatter | solution.py:133
  306.2 7.6 reshape.188
  313.8 168.2 %all_to_all.10 = bf16[64,18,2048]{2,1,0:T(8,128)(2,1)} all-to-all(bf16[64,18,2048]{2,1,0:T(8,128)(2,1)} %reshape.188), channel_id=1, replica_groups=mesh['seq'=64,'tp'=8] {'seq'}, dimensions={0} | all-to-all | bytes 9437184 | tf_op jit(solution)/shard_map/all_to_all | solution.py:136
  482.0 7.8 reshape.189
  489.8 4.2 fusion.26
  494.0 1.7 fusion.5
  495.8 1.1 copy.40
  496.8 1.4 reshape.190
  498.2 2.8 copy.41
  501.1 85.8 %all_gather.28 = bf16[2048,176]{1,0:T(8,128)(2,1)S(1)} all-gather(bf16[32,176]{1,0:T(8,128)(2,1)S(1)} %copy-done.5), channel_id=1, replica_groups=mesh['seq'=64,'tp'=8] {'seq'}, dimensions={0}, use_global_device_ids=true | all-gather | bytes 732160 | tf_op jit(solution)/shard_map/all_gather | solution.py:109
  586.8 79.7 %all_gather.29 = bf16[2048,176]{1,0:T(8,128)(2,1)S(1)} all-gather(bf16[32,176]{1,0:T(8,128)(2,1)S(1)} %copy-done.6), channel_id=1, replica_groups=mesh['seq'=64,'tp'=8] {'seq'}, dimensions={0}, use_global_device_ids=true | all-gather | bytes 732160 | tf_op jit(solution)/shard_map/all_gather | solution.py:114
  666.6 89.7 %all_gather.30 = bf16[176,2048]{0,1:T(8,128)(2,1)} all-gather(bf16[176,32]{0,1:T(8,128)(2,1)S(1)} %copy-done.7), channel_id=1, replica_groups=mesh['seq'=64,'tp'=8] {'seq'}, dimensions={1}, use_global_device_ids=true | all-gather | bytes 732160 | tf_op jit(solution)/shard_map/all_gather | solution.py:120
  756.3 0.5 fusion.47
  756.8 13.3 %copy.42 = bf16[64,18,1408]{2,1,0:T(8,128)(2,1)} copy(bf16[64,18,1408]{0,1,2:T(8,128)(2,1)} %all-gather.8.cloned.1.call-done) | data formatting | bytes 6488064 | tf_op jit(solution)/shard_map/all_gather | solution.py:22
  770.2 5.8 reshape.191
  775.9 3.8 convolution_convert_fusion
  779.8 2.1 reshape.192
  781.8 22.7 %all-to-all-start.1 = ((bf16[64,18,256]{2,1,0:T(8,128)(2,1)}), bf16[64,18,256]{2,1,0:T(8,128)(2,1)}, u32[]{:S(2)}, u32[]{:S(2)}) async-start(bf16[64,18,256]{2,1,0:T(8,128)(2,1)} %reshape.192), calls=%async_computation.2 | async-start | bytes 1572864 | tf_op jit(solution)/shard_map/all_to_all | solution.py:29
  804.6 3.2 convolution_convert_fusion.1
  807.8 1.2 fusion.48
  809.3 19.2 %all-to-all-done.1 = bf16[64,18,256]{2,1,0:T(8,128)(2,1)} async-done(((bf16[64,18,256]{2,1,0:T(8,128)(2,1)}), bf16[64,18,256]{2,1,0:T(8,128)(2,1)}, u32[]{:S(2)}, u32[]{:S(2)}) %all-to-all-start.1) | async-done | bytes 589856 | tf_op jit(solution)/shard_map/all_to_all | solution.py:29
  828.5 1.3 reshape.193
  829.8 3.3 gather_fusion
  833.1 1.1 reshape.194
  834.2 0.4 multiply_reduce_fusion
  834.6 27.8 %reduce-scatter.2.cloned.1.call-done = bf16[128,256]{1,0:T(8,128)(2,1)} async-done(((bf16[128,2048]{1,0:T(8,128)(2,1)}), bf16[128,256]{1,0:T(8,128)(2,1)}) %reduce-scatter.2.cloned.1.call-update) | async-done | bytes 65552 | tf_op jit(solution)/shard_map/reduce_scatter | solution.py:123
  862.4 1.5 add_convert_fusion
  (53 shorter events, 1.0 us)
Async XLA Ops:
  6.5 769.4 %copy-start = (bf16[1,1408,256]{2,1,0:T(8,128)(2,1)S(1)}, bf16[1,1408,256]{2,1,0:T(8,128)(2,1)}, u32[]{:S(2)}) copy-start(bf16[1,1408,256]{2,1,0:T(8,128)(2,1)} %param.30) | copy-start | bytes 2162692
  6.5 155.5 %all-gather.6.cloned.1.call-start = ((), (), s32[]{:S(2)}) async-start(), calls=%async_computation.4 | async-start | bytes 2129920 | tf_op jit(solution)/shard_map/all_gather | solution.py:60
  7.3 175.9 %all-gather.4.cloned.1.call-start = ((), (), s32[]{:S(2)}) async-start(), calls=%async_computation.3 | async-start | bytes 2129920 | tf_op jit(solution)/shard_map/all_gather | solution.py:61
  8.0 273.1 %all-reduce.2.cloned.1.call-start = ((), (), s32[]{:S(2)}) async-start(), calls=%async_computation.5 | async-start | bytes 2097152 | tf_op jit(solution)/shard_map/psum | solution.py:93
  171.6 2.1 copy-start.1
  171.6 11.5 %copy-start.11 = (bf16[128,2048]{1,0:T(8,128)(2,1)S(1)}, bf16[128,2048]{1,0:T(8,128)(2,1)}, u32[]{:S(2)}) copy-start(bf16[128,2048]{1,0:T(8,128)(2,1)} %param.24) | copy-start | bytes 1572868
  175.0 13.5 %copy-start.4 = (s32[128,6]{0,1:T(8,128)S(1)}, s32[128,6]{0,1:T(8,128)}, u32[]{:S(2)}) copy-start(s32[128,6]{0,1:T(8,128)} %param.27) | copy-start | bytes 9220
  175.0 13.9 %copy-start.8 = (bf16[2048]{0:T(1024)(128)(2,1)S(1)}, bf16[2048]{0:T(1024)(128)(2,1)}, u32[]{:S(2)}) copy-start(bf16[2048]{0:T(1024)(128)(2,1)} %param.25) | copy-start | bytes 12292
  175.0 106.1 %copy-start.3 = (bf16[128,2048]{1,0:T(8,128)(2,1)S(1)}, bf16[128,2048]{1,0:T(8,128)(2,1)}, u32[]{:S(2)}) copy-start(bf16[128,2048]{1,0:T(8,128)(2,1)} %param.17) | copy-start | bytes 1572868
  188.5 568.3 %all-gather.8.cloned.1.call-start = ((), (), s32[]{:S(2)}) async-start(), calls=%async_computation.7 | async-start | bytes 9732096 | tf_op jit(solution)/shard_map/all_gather | solution.py:22
  482.0 7.8 copy-start.9
  489.8 4.2 copy-start.2
  489.8 4.2 copy-start.10
  495.7 5.4 copy-start.5
  495.7 91.1 %copy-start.6 = (bf16[32,176]{1,0:T(8,128)(2,1)S(1)}, bf16[32,176]{1,0:T(8,128)(2,1)}, u32[]{:S(2)}) copy-start(bf16[32,176]{1,0:T(8,128)(2,1)} %param.32) | copy-start | bytes 33796
  495.7 170.8 %copy-start.7 = (bf16[176,32]{0,1:T(8,128)(2,1)S(1)}, bf16[176,32]{0,1:T(8,128)(2,1)}, u32[]{:S(2)}) copy-start(bf16[176,32]{0,1:T(8,128)(2,1)} %param.33) | copy-start | bytes 33796
  781.8 46.7 %all-to-all-start.1 = ((bf16[64,18,256]{2,1,0:T(8,128)(2,1)}), bf16[64,18,256]{2,1,0:T(8,128)(2,1)}, u32[]{:S(2)}, u32[]{:S(2)}) async-start(bf16[64,18,256]{2,1,0:T(8,128)(2,1)} %reshape.192), calls=%async_computation.2 | async-start | bytes 1572864 | tf_op jit(solution)/shard_map/all_to_all | solution.py:29
  804.5 57.9 %reduce-scatter.2.cloned.1.call-start = ((), (), s32[]{:S(2)}) async-start(), calls=%async_computation.6 | async-start | bytes 589824 | tf_op jit(solution)/shard_map/reduce_scatter | solution.py:123
Sparse Core Ops, SparseCore 0:
  10.7 88.5 all-gather.5
  102.6 80.4 all-gather.3
  188.6 92.4 all-reduce.1
  501.2 226.0 all-gather.7
  807.9 54.4 reduce-scatter.1
where the time goes:
time: 872 us; the launch traced here: 870 us
  blocking collectives  576 us (66%)
  waiting for transfers between devices  146 us (17%)
  local copies, waits for them, and re-layouts  74.3 us (9%)
  matrix products  29.6 us (3%)
  starting transfers between devices  22.9 us (3%)
  between operations  13.5 us (2%)
    all_to_all x1, blocking collectives, local(): lax.all_to_all(buffer, 'seq', split_axis=0, concat_axis=0, tiled=True)  168 us
    all_gather x1, blocking collectives, local(): lax.all_gather(w_shared_down, 'seq', axis=1, tiled=True)  89.7 us
    psum x1, waiting for transfers between devices, local(): hidden_state = resid.astype(jnp.float32) + lax.psum(partial_out, 'tp')  89.2 us
    all_gather x1, blocking collectives, local(): lax.all_gather(w_shared_gate, 'seq', axis=0, tiled=True)  85.8 us
    all_gather x1, blocking collectives, local(): lax.all_gather(w_shared_up, 'seq', axis=0, tiled=True)  79.7 us
    all_gather x1, blocking collectives, local(): lax.all_gather(key_cache, 'seq', axis=0, tiled=True)  76.9 us
    all_gather x1, blocking collectives, local(): lax.all_gather(value_cache, 'seq', axis=0, tiled=True)  75.4 us
    reduce_scatter x1, waiting for transfers between devices, local(): lax.psum_scatter(shared_terms.astype(jnp.bfloat16), 'tp', scatter_dimensi...  27.8 us
  transfers between devices with their start and end apart: 6, of which 4 were waited for; matrix products, arithmetic and copies ran while one was open for 3% of the time, Pallas kernels for 0%

commit v1 on v0

--- a/solution.py
+++ b/solution.py
@@ -90,7 +90,7 @@
     )
     attn = attn.astype(jnp.bfloat16).reshape(tok_rows, heads_here * HD)
     partial_out = jnp.dot(attn, out_weight, preferred_element_type=jnp.float32)
-    hidden_state = resid.astype(jnp.float32) + lax.psum(partial_out, "tp")
+    hidden_state = resid.astype(jnp.float32) + jnp.sum(lax.all_gather(partial_out, "tp"), axis=0)
     mean_square = jnp.mean(hidden_state * hidden_state, axis=-1, keepdims=True)
     normed = (hidden_state * lax.rsqrt(mean_square + 1e-06) * norm_gain.astype(jnp.float32)).astype(
         jnp.bfloat16

time: 872 us -> 946 us (1.085)
  the two profiles are of different devices: /device:TPU:16 before, /device:TPU:240 now
where the time goes in v1:
time: 946 us; the launch traced here: 945 us
  blocking collectives  573 us (61%)
  waiting for transfers between devices  224 us (24%)
  local copies, waits for them, and re-layouts  74 us (8%)
  matrix products  29.7 us (3%)
  starting transfers between devices  19.5 us (2%)
  between operations  13.5 us (1%)
  other arithmetic  11.3 us (1%)
    all_gather x1, waiting for transfers between devices, local(): lax.all_gather(partial_out, 'tp')  174 us
    all_to_all x1, blocking collectives, local(): lax.all_to_all(buffer, 'seq', split_axis=0, concat_axis=0, tiled=True)  168 us
    all_gather x1, blocking collectives, local(): lax.all_gather(w_shared_down, 'seq', axis=1, tiled=True)  88.6 us
    all_gather x1, blocking collectives, local(): lax.all_gather(w_shared_up, 'seq', axis=0, tiled=True)  86.6 us
    all_gather x1, blocking collectives, local(): lax.all_gather(value_cache, 'seq', axis=0, tiled=True)  79.7 us
    all_gather x1, blocking collectives, local(): lax.all_gather(w_shared_gate, 'seq', axis=0, tiled=True)  77.7 us
    all_gather x1, blocking collectives, local(): lax.all_gather(key_cache, 'seq', axis=0, tiled=True)  72.6 us
    reduce_scatter x1, waiting for transfers between devices, local(): lax.psum_scatter(shared_terms.astype(jnp.bfloat16), 'tp', scatter_dimensi...  29.9 us
  transfers between devices with their start and end apart: 6, of which 4 were waited for; matrix products, arithmetic and copies ran while one was open for 3% of the time, Pallas kernels for 0%

profile of v1, /device:TPU:240, one launch (start us, length us, event | category | flops | bytes accessed | tf_op | source)
XLA Modules:
  0.0 945.1 jit_solution(1285677586280921838)
XLA Ops:
  6.5 0.7 all-gather.8.cloned.1.call-update
  7.3 0.7 all-gather.6.cloned.1.call-update
  8.1 0.7 iota_compare_fusion.4
  8.9 72.6 %all_gather.32 = bf16[1024,128]{1,0:T(8,128)(2,1)S(1)} all-gather(bf16[16,128]{1,0:T(8,128)(2,1)} %param.21), channel_id=1, replica_groups=mesh['seq'=64,'tp'=8] {'seq'}, dimensions={0}, use_global_device_ids=true | all-gather | bytes 266240 | tf_op jit(solution)/shard_map/all_gather | solution.py:58
  81.5 79.7 %all_gather.30 = bf16[1024,128]{1,0:T(8,128)(2,1)S(1)} all-gather(bf16[16,128]{1,0:T(8,128)(2,1)} %param.22), channel_id=1, replica_groups=mesh['seq'=64,'tp'=8] {'seq'}, dimensions={0}, use_global_device_ids=true | all-gather | bytes 266240 | tf_op jit(solution)/shard_map/all_gather | solution.py:59
  161.2 0.7 iota_compare_fusion
  161.9 9.6 %fusion.46 = (f32[128]{0:T(128)S(1)}, f32[128,9216]{0,1:T(8,128)S(1)}) fusion(bf16[128,128]{1,0:T(8,128)(2,1)} %param.18, bf16[8192,128]{1,0:T(8,128)(2,1)} %all-gather.8.cloned.1.call-done, bf16[1024,128]{1,0:T(8,128)(2,1)S(1)} %all_gather.32, pred[128,8192]{0,1:T(32,128)(4,1)S(1)} %iota_compare_fusion, pred[9216]{0:T(1024)(128)(4,1)S(1)} %pad.2.clone), kind=kOutput, calls=%fused_computation.71 | convolution fusion | flops 311426944 | bytes 8168960 | tf_op jit(solution)/shard_map/qhd,khd->hqk/dot_general | solution.py:66
  171.6 2.1 copy-done.1
  173.7 1.3 fusion.2
  174.9 2.7 all-gather.6.cloned.1.call-done
  177.7 5.4 fusion.22
  183.3 0.1 eq.42
  183.7 0.1 mul.78
  183.9 0.1 reshape.187
  184.0 1.8 reduce-window.6
  185.8 0.3 slice_reduce_fusion
  186.3 174.3 %all-gather.12.cloned.1.call-done = f32[1024,2048]{1,0:T(8,128)} async-done(((f32[128,2048]{1,0:T(8,128)}), f32[1024,2048]{1,0:T(8,128)}) %all-gather.12.cloned.1.call-update) | async-done | bytes 8388624 | tf_op jit(solution)/shard_map/all_gather | solution.py:93
  360.6 4.2 reduce_sum.66
  364.8 0.2 multiply_reduce_fusion.1
  365.1 0.2 multiply_convert_fusion
  365.2 23.4 %scatter_custom_fusion = bf16[1152,2048]{1,0:T(8,128)(2,1)} fusion(s32[768]{0:T(1024)S(1)} %fusion.40, bf16[128,2048]{1,0:T(8,128)(2,1)S(1)} %multiply_convert_fusion, s32[1024]{0:T(1024)S(1)} %pad_clamp_fusion.1, bf16[]{:T(256)} %constant.44.clone.1), kind=kCustom, calls=%fused_computation.10 | custom fusion | bytes 4718594 | tf_op jit(solution)/shard_map/scatter | solution.py:133
  388.6 7.6 reshape.188
  396.2 167.9 %all_to_all.10 = bf16[64,18,2048]{2,1,0:T(8,128)(2,1)} all-to-all(bf16[64,18,2048]{2,1,0:T(8,128)(2,1)} %reshape.188), channel_id=1, replica_groups=mesh['seq'=64,'tp'=8] {'seq'}, dimensions={0} | all-to-all | bytes 9437184 | tf_op jit(solution)/shard_map/all_to_all | solution.py:136
  564.1 7.8 reshape.189
  571.9 4.2 fusion.26
  576.1 1.7 fusion.5
  577.9 1.1 copy.40
  579.0 1.4 reshape.190
  580.4 2.8 copy.41
  583.2 77.7 %all_gather.36 = bf16[2048,176]{1,0:T(8,128)(2,1)S(1)} all-gather(bf16[32,176]{1,0:T(8,128)(2,1)S(1)} %copy-done.5), channel_id=1, replica_groups=mesh['seq'=64,'tp'=8] {'seq'}, dimensions={0}, use_global_device_ids=true | all-gather | bytes 732160 | tf_op jit(solution)/shard_map/all_gather | solution.py:109
  660.9 86.6 %all_gather.37 = bf16[2048,176]{1,0:T(8,128)(2,1)S(1)} all-gather(bf16[32,176]{1,0:T(8,128)(2,1)S(1)} %copy-done.6), channel_id=1, replica_groups=mesh['seq'=64,'tp'=8] {'seq'}, dimensions={0}, use_global_device_ids=true | all-gather | bytes 732160 | tf_op jit(solution)/shard_map/all_gather | solution.py:114
  747.5 88.6 %all_gather.38 = bf16[176,2048]{0,1:T(8,128)(2,1)} all-gather(bf16[176,32]{0,1:T(8,128)(2,1)S(1)} %copy-done.7), channel_id=1, replica_groups=mesh['seq'=64,'tp'=8] {'seq'}, dimensions={1}, use_global_device_ids=true | all-gather | bytes 732160 | tf_op jit(solution)/shard_map/all_gather | solution.py:120
  836.1 0.5 fusion.47
  836.6 13.1 %copy.42 = bf16[64,18,1408]{2,1,0:T(8,128)(2,1)} copy(bf16[64,18,1408]{0,1,2:T(8,128)(2,1)} %all-gather.10.cloned.1.call-done) | data formatting | bytes 6488064 | tf_op jit(solution)/shard_map/all_gather | solution.py:22
  849.7 5.8 reshape.191
  855.5 3.8 convolution_convert_fusion
  859.3 2.1 reshape.192
  861.3 19.1 %all-to-all-start.1 = ((bf16[64,18,256]{2,1,0:T(8,128)(2,1)}), bf16[64,18,256]{2,1,0:T(8,128)(2,1)}, u32[]{:S(2)}, u32[]{:S(2)}) async-start(bf16[64,18,256]{2,1,0:T(8,128)(2,1)} %reshape.192), calls=%async_computation.2 | async-start | bytes 1572864 | tf_op jit(solution)/shard_map/all_to_all | solution.py:29
  880.4 0.3 reduce-scatter.2.cloned.1.call-start
  880.7 3.2 convolution_convert_fusion.1
  884.0 1.2 fusion.48
  885.4 15.7 %all-to-all-done.1 = bf16[64,18,256]{2,1,0:T(8,128)(2,1)} async-done(((bf16[64,18,256]{2,1,0:T(8,128)(2,1)}), bf16[64,18,256]{2,1,0:T(8,128)(2,1)}, u32[]{:S(2)}, u32[]{:S(2)}) %all-to-all-start.1) | async-done | bytes 589856 | tf_op jit(solution)/shard_map/all_to_all | solution.py:29
  901.1 1.3 reshape.193
  902.4 3.3 gather_fusion
  905.7 1.1 reshape.194
  906.8 0.4 multiply_reduce_fusion
  907.2 29.9 %reduce-scatter.2.cloned.1.call-done = bf16[128,256]{1,0:T(8,128)(2,1)} async-done(((bf16[128,2048]{1,0:T(8,128)(2,1)}), bf16[128,256]{1,0:T(8,128)(2,1)}) %reduce-scatter.2.cloned.1.call-update) | async-done | bytes 65552 | tf_op jit(solution)/shard_map/reduce_scatter | solution.py:123
  937.1 1.5 add_convert_fusion
  (54 shorter events, 1.2 us)
Async XLA Ops:
  6.5 848.9 %copy-start = (bf16[1,1408,256]{2,1,0:T(8,128)(2,1)S(1)}, bf16[1,1408,256]{2,1,0:T(8,128)(2,1)}, u32[]{:S(2)}) copy-start(bf16[1,1408,256]{2,1,0:T(8,128)(2,1)} %param.30) | copy-start | bytes 2162692
  6.5 155.4 %all-gather.8.cloned.1.call-start = ((), (), s32[]{:S(2)}) async-start(), calls=%async_computation.4 | async-start | bytes 2129920 | tf_op jit(solution)/shard_map/all_gather | solution.py:60
  7.3 170.4 %all-gather.6.cloned.1.call-start = ((), (), s32[]{:S(2)}) async-start(), calls=%async_computation.3 | async-start | bytes 2129920 | tf_op jit(solution)/shard_map/all_gather | solution.py:61
  8.0 352.6 %all-gather.12.cloned.1.call-start = ((), (), s32[]{:S(2)}) async-start(), calls=%async_computation.7 | async-start | bytes 9437184 | tf_op jit(solution)/shard_map/all_gather | solution.py:93
  171.5 2.1 copy-start.1
  171.5 6.1 copy-start.11
  174.9 8.2 copy-start.4
  174.9 8.6 copy-start.8
  183.1 653.5 %all-gather.10.cloned.1.call-start = ((), (), s32[]{:S(2)}) async-start(), calls=%async_computation.6 | async-start | bytes 9732096 | tf_op jit(solution)/shard_map/all_gather | solution.py:22
  360.6 4.2 copy-start.3
  564.1 7.8 copy-start.9
  571.9 4.2 copy-start.2
  571.9 4.2 copy-start.10
  577.9 5.4 copy-start.5
  577.9 83.0 %copy-start.6 = (bf16[32,176]{1,0:T(8,128)(2,1)S(1)}, bf16[32,176]{1,0:T(8,128)(2,1)}, u32[]{:S(2)}) copy-start(bf16[32,176]{1,0:T(8,128)(2,1)} %param.32) | copy-start | bytes 33796
  577.9 169.6 %copy-start.7 = (bf16[176,32]{0,1:T(8,128)(2,1)S(1)}, bf16[176,32]{0,1:T(8,128)(2,1)}, u32[]{:S(2)}) copy-start(bf16[176,32]{0,1:T(8,128)(2,1)} %param.33) | copy-start | bytes 33796
  861.3 39.8 %all-to-all-start.1 = ((bf16[64,18,256]{2,1,0:T(8,128)(2,1)}), bf16[64,18,256]{2,1,0:T(8,128)(2,1)}, u32[]{:S(2)}, u32[]{:S(2)}) async-start(bf16[64,18,256]{2,1,0:T(8,128)(2,1)} %reshape.192), calls=%async_computation.2 | async-start | bytes 1572864 | tf_op jit(solution)/shard_map/all_to_all | solution.py:29
  880.4 56.7 %reduce-scatter.2.cloned.1.call-start = ((), (), s32[]{:S(2)}) async-start(), calls=%async_computation.5 | async-start | bytes 589824 | tf_op jit(solution)/shard_map/reduce_scatter | solution.py:123
Sparse Core Ops, SparseCore 0:
  10.7 83.0 all-gather.7
  97.2 80.4 all-gather.5
  183.2 177.3 all-gather.11
  583.4 190.9 all-gather.9
  884.1 52.9 reduce-scatter.1
